TPU v7x, 256 devices: a whole 4x4x8 slice. The times are simulated.
256 devices in a mesh: src: 8 (over y, x_lo), lat: 32 (over x_hi, z, core).
Axes of the slice: x: 4 (x_hi: 2, x_lo: 2; x = x_hi * 2 + x_lo), y: 4, z: 8, core: 2. Of those that a mesh axis runs over, the one named last changes fastest.
Arguments:
- residual_rows: bfloat16 [1024, 8192], P(None, 'src'), may hold values from -6 to 6
- encoder: bfloat16 [8192, 32768], P('src', 'lat'), may hold values from -0.0625 to 0.0625
- decoder: bfloat16 [32768, 8192], P('lat', 'src'), may hold values from -0.0625 to 0.0625
- enc_bias: float32 [32768], P('lat'), may hold values from -3 to 3
- dec_bias: float32 [8192], P('src'), may hold values from -3 to 3
Outputs:
- grad_encoder: bfloat16 [8192, 32768], P('src', 'lat')
- grad_decoder: bfloat16 [32768, 8192], P('lat', 'src')
All inputs are finite; a program needn't handle non-finite values.
Results may differ from a plain program's by a relative error of at most 0.024.
Values may be sent and summed in bfloat16 or wider, within the bound.
No kernel may reach another device: no remote copies, remote signals or barrier semaphores. Data moves between devices by JAX's collectives and lax.ppermute only.
A program may use at most 64 MiB of HBM per device.

v0:
```python
import math

import jax
import jax.numpy as jnp
from jax import lax
from jax.sharding import PartitionSpec as P

D = 4096
SRCS = 2


SHARPNESS = 8.0
PENALTY = 1.0
EPSILON = 1e-06


def per_device(residual_rows, encoder, decoder, enc_bias, dec_bias):
    row_count = residual_rows.shape[0]
    feat_dev = residual_rows.shape[1]
    loss_scale = 1.0 / math.sqrt(row_count)
    owner_src = lax.axis_index("src") // (D // feat_dev)
    source_mask = jnp.arange(SRCS) == owner_src
    squares = jnp.sum(jnp.square(decoder.astype(jnp.float32)), axis=1)
    slots = jnp.where(source_mask[:, None], squares[None, :], 0.0)
    norm_sq = lax.psum(slots, "src")
    dec_norms = jnp.sqrt(norm_sq + EPSILON)
    penalty = PENALTY * jnp.sum(dec_norms, axis=0)
    own_norm = jnp.sum(jnp.where(source_mask[:, None], dec_norms, 0.0), axis=0)
    pre_act = (
        lax.psum(
            jnp.dot(residual_rows, encoder, preferred_element_type=jnp.float32).astype(
                jnp.bfloat16
            ),
            "src",
        ).astype(jnp.float32)
        + enc_bias[None, :]
    )
    latent_act = (jax.nn.softplus(SHARPNESS * pre_act) / SHARPNESS).astype(jnp.bfloat16)
    gate_slope = jax.nn.sigmoid(SHARPNESS * pre_act)
    recon = (
        lax.psum(
            jnp.dot(latent_act, decoder, preferred_element_type=jnp.float32).astype(jnp.bfloat16),
            "lat",
        ).astype(jnp.float32)
        + dec_bias[None, :]
    )
    errors = (recon - residual_rows.astype(jnp.float32)).astype(jnp.bfloat16)
    col_sums = jnp.sum(latent_act.astype(jnp.float32), axis=0)
    outer = jnp.einsum("bj,bk->jk", latent_act, errors, preferred_element_type=jnp.float32)
    shrink = loss_scale * PENALTY * col_sums / own_norm
    grad_decoder = (loss_scale * outer + shrink[:, None] * decoder.astype(jnp.float32)).astype(
        jnp.bfloat16
    )
    act_grad = lax.psum(
        jnp.einsum("bk,jk->bj", errors, decoder, preferred_element_type=jnp.float32).astype(
            jnp.bfloat16
        ),
        "src",
    ).astype(jnp.float32)
    grad_pre = (loss_scale * (act_grad + penalty[None, :]) * gate_slope).astype(jnp.bfloat16)
    grad_encoder = jnp.einsum(
        "bk,bj->kj", residual_rows, grad_pre, preferred_element_type=jnp.float32
    ).astype(jnp.bfloat16)
    return (grad_encoder, grad_decoder)


def solution(mesh):
    in_specs = (P(None, "src"), P("src", "lat"), P("lat", "src"), P("lat"), P("src"))
    out_specs = (P("src", "lat"), P("lat", "src"))
    return jax.shard_map(
        per_device, mesh=mesh, in_specs=in_specs, out_specs=out_specs, check_vma=False
    )
```

profile of v0, /device:TPU:32, one launch (start us, length us, event | category | flops | bytes accessed | tf_op | source)
XLA Modules:
  0.0 538.2 jit_solution(3028635346419425493)
XLA Ops:
  7.2 0.0 copy-start
  7.2 0.0 all-reduce.4.cloned.1.call-start
  7.2 1.5 copy-done
  8.8 5.2 convolution_convert_fusion.2
  14.0 0.0 copy-start.3
  14.0 0.0 all-reduce.4.cloned.1.call-update
  14.0 0.0 all-reduce.6.cloned.1.call-start
  14.1 112.4 %all-reduce.4.cloned.1.call-done = bf16[1024,1024]{1,0:T(8,128)(2,1)} async-done(((bf16[1024,1024]{1,0:T(8,128)(2,1)}), bf16[1024,1024]{1,0:T(8,128)(2,1)}) %all-reduce.4.cloned.1.call-update) | async-done | bytes 2097168 | tf_op jit(solution)/shard_map/psum | solution.py:30
  126.5 0.0 copy-done.3
  126.5 8.0 %convolution_convert_fusion.1 = bf16[1024,1024]{1,0:T(8,128)(2,1)} fusion(bf16[1024,1024]{1,0:T(8,128)(2,1)} %param.7, bf16[1024,1024]{1,0:T(8,128)(2,1)} %all-reduce.4.cloned.1.call-done, f32[1024]{0:T(1024)S(1)} %copy-done.3), kind=kOutput, calls=%fused_computation.15 | convolution fusion | flops 2160066560 | bytes 6295552 | tf_op jit(solution)/shard_map/dot_general | solution.py:42
  134.5 0.0 copy-start.2
  134.5 0.0 all-reduce.6.cloned.1.call-update
  134.5 0.0 all-reduce.8.cloned.1.call-start
  134.6 2.1 fusion
  136.6 263.7 %all-reduce.6.cloned.1.call-done = bf16[1024,1024]{1,0:T(8,128)(2,1)} async-done(((bf16[1024,1024]{1,0:T(8,128)(2,1)}), bf16[1024,1024]{1,0:T(8,128)(2,1)}) %all-reduce.6.cloned.1.call-update) | async-done | bytes 2097168 | tf_op jit(solution)/shard_map/psum | solution.py:41
  400.3 0.0 copy-done.2
  400.3 6.6 %convolution_convert_fusion = bf16[1024,1024]{1,0:T(8,128)(2,1)} fusion(bf16[1024,1024]{1,0:T(8,128)(2,1)} %param.7, bf16[1024,1024]{1,0:T(8,128)(2,1)} %param.5, bf16[1024,1024]{1,0:T(8,128)(2,1)} %all-reduce.6.cloned.1.call-done, f32[1024]{0:T(1024)S(1)} %copy-done.2), kind=kOutput, calls=%fused_computation.14 | convolution fusion | flops 2153775104 | bytes 8392704 | tf_op jit(solution)/shard_map/bk,jk->bj/dot_general | solution.py:55
  406.9 0.0 all-reduce.8.cloned.1.call-update
  406.9 0.1 broadcast_select_fusion
  407.0 19.6 %psum.31 = f32[2,1024]{1,0:T(2,128)S(1)} all-reduce(f32[2,1024]{1,0:T(2,128)S(1)} %broadcast_select_fusion), channel_id=1, replica_groups=mesh['src'=8,'lat'=32] {'src'}, use_global_device_ids=true, to_apply=%region_4.5 | all-reduce | flops 2048 | bytes 16384 | tf_op jit(solution)/shard_map/psum | solution.py:25
  426.6 0.0 copy-start.1
  426.6 0.1 select_reduce_fusion
  426.7 4.6 convert_reduce_fusion
  431.3 0.0 copy-done.1
  431.3 9.6 %fusion.2 = bf16[1024,1024]{1,0:T(8,128)(2,1)} fusion(bf16[1024,1024]{1,0:T(8,128)(2,1)S(1)} %copy-done.1, f32[1024]{0:T(1024)S(1)} %multiply_divide_fusion, bf16[1024,1024]{1,0:T(8,128)(2,1)} %param.5, bf16[1024,1024]{1,0:T(8,128)(2,1)} %all-reduce.6.cloned.1.call-done, f32[1024]{0:T(1024)S(1)} %copy-done.2, ...), kind=kOutput, calls=%fused_computation.5 | convolution fusion | flops 2169503744 | bytes 10498048 | tf_op jit(solution)/shard_map/bj,bk->jk/dot_general | solution.py:49
  440.9 79.3 %all-reduce.8.cloned.1.call-done = bf16[1024,1024]{1,0:T(8,128)(2,1)} async-done(((bf16[1024,1024]{1,0:T(8,128)(2,1)}), bf16[1024,1024]{1,0:T(8,128)(2,1)}) %all-reduce.8.cloned.1.call-update) | async-done | bytes 2097168 | tf_op jit(solution)/shard_map/psum | solution.py:54
  520.2 7.5 %convert_bitcast_fusion = bf16[1024,1024]{0,1:T(8,128)(2,1)} fusion(bf16[1024,1024]{1,0:T(8,128)(2,1)} %param.5, bf16[1024,1024]{1,0:T(8,128)(2,1)} %all-reduce.8.cloned.1.call-done, bf16[1024,1024]{1,0:T(8,128)(2,1)} %all-reduce.4.cloned.1.call-done, f32[1024]{0:T(1024)S(1)} %get-tuple-element.7, f32[1024]{0:T(1024)S(1)} %copy-done.3), kind=kOutput, calls=%fused_computation.12 | convolution fusion | flops 2160066560 | bytes 8396800 | tf_op jit(solution)/shard_map/bk,bj->kj/dot_general | solution.py:61
  527.7 3.9 copy.8
  (2 shorter events, 0.0 us)
Async XLA Ops:
  7.2 1.6 copy-start
  7.2 119.3 %all-reduce.4.cloned.1.call-start = ((), (), s32[]{:S(2)}) async-start(), calls=%async_computation | async-start | bytes 4194304 | tf_op jit(solution)/shard_map/psum | solution.py:30
  14.0 112.5 %copy-start.3 = (f32[1024]{0:T(1024)S(1)}, f32[1024]{0:T(1024)}, u32[]{:S(2)}) copy-start(f32[1024]{0:T(1024)} %param.8) | copy-start | bytes 12292
  14.0 386.3 %all-reduce.6.cloned.1.call-start = ((), (), s32[]{:S(2)}) async-start(), calls=%async_computation.1 | async-start | bytes 4194304 | tf_op jit(solution)/shard_map/psum | solution.py:41
  134.5 265.8 %copy-start.2 = (f32[1024]{0:T(1024)S(1)}, f32[1024]{0:T(1024)}, u32[]{:S(2)}) copy-start(f32[1024]{0:T(1024)} %param.9) | copy-start | bytes 12292
  134.5 385.7 %all-reduce.8.cloned.1.call-start = ((), (), s32[]{:S(2)}) async-start(), calls=%async_computation.2 | async-start | bytes 4194304 | tf_op jit(solution)/shard_map/psum | solution.py:54
  426.6 4.7 copy-start.1
Sparse Core Ops, SparseCore 0:
  14.1 112.3 all-reduce.3
  134.6 265.6 all-reduce.5
  407.0 113.1 all-reduce.7
where the time goes:
time: 539 us; the launch traced here: 538 us
  waiting for transfers between devices  455 us (84%)
  matrix products  36.8 us (7%)
  blocking collectives  19.6 us (4%)
  between operations  13.8 us (3%)
  other arithmetic  6.83 us (1%)
  local copies, waits for them, and re-layouts  5.49 us (1%)
    psum x1, waiting for transfers between devices, per_device(): lax.psum(jnp.dot(latent_act, decoder, preferred_element_type=jnp.float32)...  264 us
    psum x1, waiting for transfers between devices, per_device(): lax.psum(jnp.dot(residual_rows, encoder, preferred_element_type=jnp.float...  112 us
    psum x1, waiting for transfers between devices, per_device(): lax.psum(jnp.einsum('bk,jk->bj', errors, decoder, preferred_element_type=...  79.3 us
    psum x1, blocking collectives, per_device(): norm_sq = lax.psum(slots, 'src')  19.6 us
  transfers between devices with their start and end apart: 3, of which 3 were waited for; matrix products, arithmetic and copies ran while one was open for 3% of the time, Pallas kernels for 0%

commit v1 on v0

v1 whole, which is shorter than its diff:
```python
import math

import jax
import jax.numpy as jnp
from jax import lax
from jax.sharding import Mesh
from jax.sharding import PartitionSpec as P

D = 4096
SRCS = 2

SHARPNESS = 8.0
PENALTY = 1.0
EPSILON = 1e-06

SRC = ("y", "xl")
LAT = ("xh", "z", "core")
RING = ("xh", "z")
CHUNKS = 2


def swap(value, axis, size, mask):
    return lax.ppermute(value, axis, [(i, i ^ mask) for i in range(size)])


def scatter_sum(partial, axes, size):
    rows = partial.shape[0] // size
    got = lax.all_to_all(partial.reshape(size, rows, -1), axes, 0, 0)
    return jnp.sum(got.astype(jnp.float32), axis=0)


def gather(shard, axes, size):
    got = lax.all_to_all(jnp.broadcast_to(shard[None], (size,) + shard.shape), axes, 0, 0)
    return got.reshape(size * shard.shape[0], -1)


def make_per_device(sizes):
    n_y, n_xl, n_xh, n_z, n_core = (sizes[a] for a in ("y", "xl", "xh", "z", "core"))
    n_src = n_y * n_xl
    n_ring = n_xh * n_z

    def per_device(residual_rows, encoder, decoder, enc_bias, dec_bias):
        row_count, feat_dev = residual_rows.shape
        loss_scale = 1.0 / math.sqrt(row_count)
        chunk = row_count // CHUNKS
        half = chunk // n_core
        core = lax.axis_index("core")
        ring = lax.axis_index(RING)

        squares = jnp.sum(jnp.square(decoder.astype(jnp.float32)), axis=1)
        own_sq = squares + swap(squares, "xl", n_xl, 1)
        own_sq = own_sq + swap(own_sq, "y", n_y, 1)
        other_sq = swap(own_sq, "y", n_y, 2)
        own_norm = jnp.sqrt(own_sq + EPSILON)
        penalty = PENALTY * (own_norm + jnp.sqrt(other_sq + EPSILON))

        chunks = [slice(i * chunk, (i + 1) * chunk) for i in range(CHUNKS)]
        latents, slopes, all_errors, grads = [], [], [], []
        for rows in chunks:
            partial = jnp.dot(
                residual_rows[rows], encoder, preferred_element_type=jnp.float32
            ).astype(jnp.bfloat16)
            pre_act = scatter_sum(partial, SRC, n_src) + enc_bias[None, :]
            latent = (jax.nn.softplus(SHARPNESS * pre_act) / SHARPNESS).astype(jnp.bfloat16)
            slopes.append(jax.nn.sigmoid(SHARPNESS * pre_act))
            latents.append(gather(latent, SRC, n_src))
        for i, rows in enumerate(chunks):
            halves = latents[i].reshape(n_core, half, -1)
            theirs = jnp.dot(
                lax.dynamic_index_in_dim(halves, 1 - core, 0, False),
                decoder,
                preferred_element_type=jnp.float32,
            ).astype(jnp.bfloat16)
            theirs = swap(theirs, "core", n_core, 1)
            mine = jnp.dot(
                lax.dynamic_index_in_dim(halves, core, 0, False),
                decoder,
                preferred_element_type=jnp.float32,
            )
            mine = (mine + theirs.astype(jnp.float32)).astype(jnp.bfloat16)
            recon = scatter_sum(mine, RING, n_ring) + dec_bias[None, :]
            own = half // n_ring
            target = lax.dynamic_slice_in_dim(
                residual_rows, rows.start + core * half + ring * own, own, 0
            )
            errors = (recon - target.astype(jnp.float32)).astype(jnp.bfloat16)
            errors = gather(errors, RING, n_ring)
            other = swap(errors, "core", n_core, 1)
            first = core == 0
            errors = jnp.concatenate(
                [jnp.where(first, errors, other), jnp.where(first, other, errors)], axis=0
            )
            all_errors.append(errors)
        for i, rows in enumerate(chunks):
            back = jnp.einsum(
                "bk,jk->bj", all_errors[i], decoder, preferred_element_type=jnp.float32
            ).astype(jnp.bfloat16)
            act_grad = scatter_sum(back, SRC, n_src)
            grad_pre = (loss_scale * (act_grad + penalty[None, :]) * slopes[i]).astype(jnp.bfloat16)
            grads.append(gather(grad_pre, SRC, n_src))
        latent_act = jnp.concatenate(latents, axis=0)
        errors = jnp.concatenate(all_errors, axis=0)
        grad_pre = jnp.concatenate(grads, axis=0)
        col_sums = jnp.sum(latent_act.astype(jnp.float32), axis=0)
        outer = jnp.einsum("bj,bk->jk", latent_act, errors, preferred_element_type=jnp.float32)
        shrink = loss_scale * PENALTY * col_sums / own_norm
        grad_decoder = (
            loss_scale * outer + shrink[:, None] * decoder.astype(jnp.float32)
        ).astype(jnp.bfloat16)
        grad_encoder = jnp.einsum(
            "bk,bj->kj", residual_rows, grad_pre, preferred_element_type=jnp.float32
        ).astype(jnp.bfloat16)
        return (grad_encoder, grad_decoder)

    return per_device


def solution(mesh):
    names = ("y", "xl", "xh", "z", "core")
    shape = (4, 2, 2, 8, 2)
    fine = Mesh(mesh.devices.reshape(shape), names)
    in_specs = (P(None, SRC), P(SRC, LAT), P(LAT, SRC), P(LAT), P(SRC))
    out_specs = (P(SRC, LAT), P(LAT, SRC))
    return jax.shard_map(
        make_per_device(dict(zip(names, shape))),
        mesh=fine,
        in_specs=in_specs,
        out_specs=out_specs,
        check_vma=False,
    )
```

time: 539 us -> 268 us (0.50)
  waiting for transfers between devices: 455 us -> 111 us
  starting transfers between devices: 0.12 us -> 58.3 us
  blocking collectives: 19.6 us -> 35.7 us
  between operations: 13.8 us -> 0.88 us
  local copies, waits for them, and re-layouts: 5.49 us -> 13.5 us
    psum x3 -> x0, waiting for transfers between devices: 455 us -> none  [the longest x1 264 us: per_device(): lax.psum(jnp.dot(latent_act, decoder, preferred_element_type=jnp.float32)...]
    all_to_all x0 -> x10, waiting for transfers between devices: none -> 95.9 us  [the longest x6 57.8 us: scatter_sum(): got = lax.all_to_all(partial.reshape(size, rows, -1), axes, 0, 0)]
    all_to_all x0 -> x10, starting transfers between devices: none -> 52.1 us  [the longest x6 34.6 us: scatter_sum(): got = lax.all_to_all(partial.reshape(size, rows, -1), axes, 0, 0)]
    all_to_all x0 -> x2, blocking collectives: none -> 35.7 us  [gather(): lax.all_to_all(jnp.broadcast_to(shard[None], (size,) + shard.shape), axes...]
    psum x1 -> x0, blocking collectives: 19.6 us -> none  [per_device(): norm_sq = lax.psum(slots, 'src')]
    ppermute x0 -> x7, waiting for transfers between devices: none -> 15.2 us  [swap(): return lax.ppermute(value, axis, [(i, i ^ mask) for i in range(size)])]
    ppermute x0 -> x7, starting transfers between devices: none -> 6.18 us  [swap(): return lax.ppermute(value, axis, [(i, i ^ mask) for i in range(size)])]
    dot_general x3 -> x8, matrix products: 19.7 us -> 22.9 us  [the longest x2 6.89 us: per_device(): jnp.dot(residual_rows[rows], encoder, preferred_element_type=jnp.float32)]
  transfers between devices with their start and end apart: 3 -> 17, of which waited for: 3 -> 14; matrix products, arithmetic and copies ran while one was open for 3% -> 12% of each run, Pallas kernels for 0% -> 0%
where the time goes in v1:
time: 268 us; the launch traced here: 266 us
  waiting for transfers between devices  111 us (41%)
  starting transfers between devices  58.3 us (22%)
  blocking collectives  35.7 us (13%)
  matrix products  35.3 us (13%)
  local copies, waits for them, and re-layouts  13.5 us (5%)
  other arithmetic  11.7 us (4%)
    all_to_all x6, waiting for transfers between devices, scatter_sum(): got = lax.all_to_all(partial.reshape(size, rows, -1), axes, 0, 0)  57.8 us
    all_to_all x4, waiting for transfers between devices, gather(): lax.all_to_all(jnp.broadcast_to(shard[None], (size,) + shard.shape), axes...  38.1 us
    all_to_all x2, blocking collectives, gather(): lax.all_to_all(jnp.broadcast_to(shard[None], (size,) + shard.shape), axes...  35.7 us
    all_to_all x6, starting transfers between devices, scatter_sum(): got = lax.all_to_all(partial.reshape(size, rows, -1), axes, 0, 0)  34.6 us
    all_to_all x4, starting transfers between devices, gather(): lax.all_to_all(jnp.broadcast_to(shard[None], (size,) + shard.shape), axes...  17.5 us
    ppermute x7, waiting for transfers between devices, swap(): return lax.ppermute(value, axis, [(i, i ^ mask) for i in range(size)])  15.2 us
    unnamed x29, local copies, waits for them, and re-layouts  9.05 us
    dot_general x2, matrix products, per_device(): jnp.dot(residual_rows[rows], encoder, preferred_element_type=jnp.float32)  6.89 us
  transfers between devices with their start and end apart: 17, of which 14 were waited for; matrix products, arithmetic and copies ran while one was open for 12% of the time, Pallas kernels for 0%

profile of v1, /device:TPU:32, one launch (start us, length us, event | category | flops | bytes accessed | tf_op | source)
XLA Modules:
  0.0 266.5 jit_solution(16236815372868738518)
XLA Ops:
  2.2 3.4 %convolution_convert_fusion.1 = bf16[512,1024]{1,0:T(8,128)(2,1)} fusion(bf16[1024,1024]{1,0:T(8,128)(2,1)S(1)} %copy-done, bf16[1024,1024]{1,0:T(8,128)(2,1)} %param.5), kind=kOutput, calls=%fused_computation.25 | convolution fusion | flops 1074266112 | bytes 4194304 | tf_op jit(solution)/shard_map/dot_general | solution.py:60
  5.7 5.4 %all-to-all-start.6 = ((bf16[8,64,1024]{2,1,0:T(8,128)(2,1)}), bf16[8,64,1024]{2,1,0:T(8,128)(2,1)S(1)}, u32[]{:S(2)}, u32[]{:S(2)}) async-start(bf16[8,64,1024]{2,1,0:T(8,128)(2,1)} %bitcast.54), calls=%async_computation.6 | async-start | bytes 2097152 | tf_op jit(solution)/shard_map/all_to_all | solution.py:28
  11.1 3.4 %convolution_convert_fusion.3 = bf16[512,1024]{1,0:T(8,128)(2,1)} fusion(bf16[1024,1024]{1,0:T(8,128)(2,1)S(1)} %copy-done, bf16[1024,1024]{1,0:T(8,128)(2,1)} %param.5), kind=kOutput, calls=%fused_computation.27 | convolution fusion | flops 1074266112 | bytes 4194304 | tf_op jit(solution)/shard_map/dot_general | solution.py:60
  14.5 12.3 %all-to-all-done.6 = bf16[8,64,1024]{2,1,0:T(8,128)(2,1)S(1)} async-done(((bf16[8,64,1024]{2,1,0:T(8,128)(2,1)}), bf16[8,64,1024]{2,1,0:T(8,128)(2,1)S(1)}, u32[]{:S(2)}, u32[]{:S(2)}) %all-to-all-start.6) | async-done | bytes 1048608 | tf_op jit(solution)/shard_map/all_to_all | solution.py:28
  26.8 4.4 %all-to-all-start = ((bf16[8,64,1024]{2,1,0:T(8,128)(2,1)}), bf16[8,64,1024]{2,1,0:T(8,128)(2,1)}, u32[]{:S(2)}, u32[]{:S(2)}) async-start(bf16[8,64,1024]{2,1,0:T(8,128)(2,1)} %bitcast.53), calls=%async_computation | async-start | bytes 2097152 | tf_op jit(solution)/shard_map/all_to_all | solution.py:28
  31.3 14.4 %all-to-all-done = bf16[8,64,1024]{2,1,0:T(8,128)(2,1)} async-done(((bf16[8,64,1024]{2,1,0:T(8,128)(2,1)}), bf16[8,64,1024]{2,1,0:T(8,128)(2,1)}, u32[]{:S(2)}, u32[]{:S(2)}) %all-to-all-start) | async-done | bytes 1048608 | tf_op jit(solution)/shard_map/all_to_all | solution.py:28
  49.3 3.6 %all-to-all-start.1 = ((bf16[8,64,1024]{2,1,0:T(8,128)(2,1)}), bf16[8,64,1024]{2,1,0:T(8,128)(2,1)S(1)}, u32[]{:S(2)}, u32[]{:S(2)}) async-start(bf16[8,64,1024]{2,1,0:T(8,128)(2,1)} %broadcast_in_dim.12), calls=%async_computation.1 | async-start | bytes 2097152 | tf_op jit(solution)/shard_map/all_to_all | solution.py:33
  52.8 13.6 %all-to-all-done.1 = bf16[8,64,1024]{2,1,0:T(8,128)(2,1)S(1)} async-done(((bf16[8,64,1024]{2,1,0:T(8,128)(2,1)}), bf16[8,64,1024]{2,1,0:T(8,128)(2,1)S(1)}, u32[]{:S(2)}, u32[]{:S(2)}) %all-to-all-start.1) | async-done | bytes 1048608 | tf_op jit(solution)/shard_map/all_to_all | solution.py:33
  67.7 4.2 %all-to-all-start.7 = ((bf16[8,64,1024]{2,1,0:T(8,128)(2,1)}), bf16[8,64,1024]{2,1,0:T(8,128)(2,1)}, u32[]{:S(2)}, u32[]{:S(2)}) async-start(bf16[8,64,1024]{2,1,0:T(8,128)(2,1)} %broadcast_in_dim.15), calls=%async_computation.7 | async-start | bytes 2097152 | tf_op jit(solution)/shard_map/all_to_all | solution.py:33
  71.9 3.1 %convolution_convert_fusion.5 = bf16[256,1024]{1,0:T(8,128)(2,1)} fusion(bf16[1024,1024]{1,0:T(8,128)(2,1)} %param.7, bf16[2,256,1024]{2,1,0:T(8,128)(2,1)S(1)} %bitcast.45, s32[]{:T(128)S(6)} %select_n.53), kind=kOutput, calls=%fused_computation.29 | convolution fusion | flops 537133056 | bytes 3145732 | tf_op jit(solution)/shard_map/dot_general | solution.py:69
  77.3 3.2 %add_convert_fusion.1 = bf16[256,1024]{1,0:T(8,128)(2,1)} fusion(bf16[256,1024]{1,0:T(8,128)(2,1)} %collective-permute-done, bf16[1024,1024]{1,0:T(8,128)(2,1)} %param.7, bf16[2,256,1024]{2,1,0:T(8,128)(2,1)S(1)} %bitcast.46, s32[]{:T(128)S(6)} %select_n.52), kind=kOutput, calls=%fused_computation.40 | convolution fusion | flops 537657344 | bytes 3670020 | tf_op jit(solution)/shard_map/dot_general | solution.py:75
  80.5 4.2 %all-to-all-done.7 = bf16[8,64,1024]{2,1,0:T(8,128)(2,1)} async-done(((bf16[8,64,1024]{2,1,0:T(8,128)(2,1)}), bf16[8,64,1024]{2,1,0:T(8,128)(2,1)}, u32[]{:S(2)}, u32[]{:S(2)}) %all-to-all-start.7) | async-done | bytes 1048608 | tf_op jit(solution)/shard_map/all_to_all | solution.py:33
  84.7 10.8 %all-to-all-start.2 = ((bf16[16,16,1024]{2,1,0:T(8,128)(2,1)}), bf16[16,16,1024]{2,1,0:T(8,128)(2,1)S(1)}, u32[]{:S(2)}, u32[]{:S(2)}) async-start(bf16[16,16,1024]{2,1,0:T(8,128)(2,1)} %bitcast.56), calls=%async_computation.2 | async-start | bytes 1048576 | tf_op jit(solution)/shard_map/all_to_all | solution.py:28
  95.5 2.6 convolution_convert_fusion.4
  100.1 2.5 add_convert_fusion
  102.7 5.4 %all-to-all-done.2 = bf16[16,16,1024]{2,1,0:T(8,128)(2,1)S(1)} async-done(((bf16[16,16,1024]{2,1,0:T(8,128)(2,1)}), bf16[16,16,1024]{2,1,0:T(8,128)(2,1)S(1)}, u32[]{:S(2)}, u32[]{:S(2)}) %all-to-all-start.2) | async-done | bytes 524320 | tf_op jit(solution)/shard_map/all_to_all | solution.py:28
  108.1 5.3 %all-to-all-start.8 = ((bf16[16,16,1024]{2,1,0:T(8,128)(2,1)}), bf16[16,16,1024]{2,1,0:T(8,128)(2,1)S(1)}, u32[]{:S(2)}, u32[]{:S(2)}) async-start(bf16[16,16,1024]{2,1,0:T(8,128)(2,1)} %bitcast.55), calls=%async_computation.8 | async-start | bytes 1048576 | tf_op jit(solution)/shard_map/all_to_all | solution.py:28
  113.4 15.8 %all-to-all-done.8 = bf16[16,16,1024]{2,1,0:T(8,128)(2,1)S(1)} async-done(((bf16[16,16,1024]{2,1,0:T(8,128)(2,1)}), bf16[16,16,1024]{2,1,0:T(8,128)(2,1)S(1)}, u32[]{:S(2)}, u32[]{:S(2)}) %all-to-all-start.8) | async-done | bytes 524320 | tf_op jit(solution)/shard_map/all_to_all | solution.py:28
  130.2 20.1 %all_to_all.60 = bf16[16,16,1024]{2,1,0:T(8,128)(2,1)S(1)} all-to-all(bf16[16,16,1024]{2,1,0:T(8,128)(2,1)S(1)} %broadcast_in_dim.16), channel_id=1, replica_groups=mesh['y'=4,'xl'=2,'xh'=2,'z'=8,'core'=2] {'xh','z'}, dimensions={0} | all-to-all | bytes 1048576 | tf_op jit(solution)/shard_map/all_to_all | solution.py:33
  151.1 5.5 %all-to-all-start.3 = ((bf16[16,16,1024]{2,1,0:T(8,128)(2,1)}), bf16[16,16,1024]{2,1,0:T(8,128)(2,1)}, u32[]{:S(2)}, u32[]{:S(2)}) async-start(bf16[16,16,1024]{2,1,0:T(8,128)(2,1)} %broadcast_in_dim.13), calls=%async_computation.3 | async-start | bytes 1048576 | tf_op jit(solution)/shard_map/all_to_all | solution.py:33
  156.6 15.2 %all-to-all-done.3 = bf16[16,16,1024]{2,1,0:T(8,128)(2,1)} async-done(((bf16[16,16,1024]{2,1,0:T(8,128)(2,1)}), bf16[16,16,1024]{2,1,0:T(8,128)(2,1)}, u32[]{:S(2)}, u32[]{:S(2)}) %all-to-all-start.3) | async-done | bytes 524320 | tf_op jit(solution)/shard_map/all_to_all | solution.py:33
  176.0 4.4 %all-to-all-start.10 = ((bf16[8,64,1024]{2,1,0:T(8,128)(2,1)}), bf16[8,64,1024]{2,1,0:T(8,128)(2,1)S(1)}, u32[]{:S(2)}, u32[]{:S(2)}) async-start(bf16[8,64,1024]{2,1,0:T(8,128)(2,1)} %bitcast.52), calls=%async_computation.10 | async-start | bytes 2097152 | tf_op jit(solution)/shard_map/all_to_all | solution.py:28
  185.2 9.9 %all-to-all-done.10 = bf16[8,64,1024]{2,1,0:T(8,128)(2,1)S(1)} async-done(((bf16[8,64,1024]{2,1,0:T(8,128)(2,1)}), bf16[8,64,1024]{2,1,0:T(8,128)(2,1)S(1)}, u32[]{:S(2)}, u32[]{:S(2)}) %all-to-all-start.10) | async-done | bytes 1048608 | tf_op jit(solution)/shard_map/all_to_all | solution.py:28
  195.1 4.4 %all-to-all-start.4 = ((bf16[8,64,1024]{2,1,0:T(8,128)(2,1)}), bf16[8,64,1024]{2,1,0:T(8,128)(2,1)}, u32[]{:S(2)}, u32[]{:S(2)}) async-start(bf16[8,64,1024]{2,1,0:T(8,128)(2,1)} %bitcast.50), calls=%async_computation.4 | async-start | bytes 2097152 | tf_op jit(solution)/shard_map/all_to_all | solution.py:28
  203.6 7.9 %collective-permute-done.2 = f32[1024]{0:T(1024)S(1)} collective-permute-done((f32[1024]{0:T(1024)S(1)}, f32[1024]{0:T(1024)S(1)}, u32[]{:S(2)}, u32[]{:S(2)}) %collective-permute-start.2) | collective-permute-done | bytes 4128 | tf_op jit(solution)/shard_map/ppermute | solution.py:23
  215.2 3.1 %collective-permute-start.4 = (f32[1024]{0:T(1024)S(1)}, f32[1024]{0:T(1024)S(1)}, u32[]{:S(2)}, u32[]{:S(2)}) collective-permute-start(f32[1024]{0:T(1024)S(1)} %get-tuple-element.7), channel_id=1, source_target_pairs={{0,128},{64,192},{128,0},{192,64},{1,129},{65,193},{129,1},{193,65... | collective-permute-start | bytes 12296 | tf_op jit(solution)/shard_map/ppermute | solution.py:23
  224.0 15.7 %all_to_all.61 = bf16[8,64,1024]{2,1,0:T(8,128)(2,1)} all-to-all(bf16[8,64,1024]{2,1,0:T(8,128)(2,1)S(1)} %broadcast_in_dim.14), channel_id=1, replica_groups=mesh['y'=4,'xl'=2,'xh'=2,'z'=8,'core'=2] {'y','xl'}, dimensions={0} | all-to-all | bytes 2097152 | tf_op jit(solution)/shard_map/all_to_all | solution.py:33
  240.8 4.2 %all-to-all-start.11 = ((bf16[8,64,1024]{2,1,0:T(8,128)(2,1)}), bf16[8,64,1024]{2,1,0:T(8,128)(2,1)}, u32[]{:S(2)}, u32[]{:S(2)}) async-start(bf16[8,64,1024]{2,1,0:T(8,128)(2,1)} %broadcast_in_dim.17), calls=%async_computation.11 | async-start | bytes 2097152 | tf_op jit(solution)/shard_map/all_to_all | solution.py:33
  245.0 6.5 %fusion.2 = bf16[1024,1024]{1,0:T(8,128)(2,1)} fusion(bf16[1024,1024]{1,0:T(8,128)(2,1)} %param.7, f32[1024]{0:T(1024)S(1)} %get-tuple-element.6, bf16[256,1024]{1,0:T(8,128)(2,1)} %copy-done.9, bf16[256,1024]{1,0:T(8,128)(2,1)} %copy-done.8, bf16[256,1024]{1,0:T(8,128)(2,1)} %copy-done.11, bf16[256,1024]{1,0:T(8,128)(2,1)} %copy-done.10, ...), kind=kOutput, calls=%fused_computation.4 | convolution fusion | flops 2165309440 | bytes 8392704 | tf_op jit(solution)/shard_map/bj,bk->jk/dot_general | solution.py:105
  251.5 5.0 %all-to-all-done.11 = bf16[8,64,1024]{2,1,0:T(8,128)(2,1)} async-done(((bf16[8,64,1024]{2,1,0:T(8,128)(2,1)}), bf16[8,64,1024]{2,1,0:T(8,128)(2,1)}, u32[]{:S(2)}, u32[]{:S(2)}) %all-to-all-start.11) | async-done | bytes 1048608 | tf_op jit(solution)/shard_map/all_to_all | solution.py:33
  256.6 5.9 %convert_bitcast_fusion = bf16[1024,1024]{0,1:T(8,128)(2,1)} fusion(bf16[1024,1024]{1,0:T(8,128)(2,1)} %param.5, bf16[512,1024]{1,0:T(8,128)(2,1)} %bitcast.15, bf16[512,1024]{1,0:T(8,128)(2,1)} %bitcast.51), kind=kOutput, calls=%fused_computation.19 | convolution fusion | flops 2152726528 | bytes 6291456 | tf_op jit(solution)/shard_map/bk,bj->kj/dot_general | solution.py:110
  262.5 3.9 %copy.8 = bf16[1024,1024]{1,0:T(8,128)(2,1)} copy(bf16[1024,1024]{0,1:T(8,128)(2,1)} %convert_bitcast_fusion) | data formatting | bytes 4194304
  (65 shorter events, 36.1 us)
Async XLA Ops:
  0.6 1.6 copy-start
  5.7 21.1 %all-to-all-start.6 = ((bf16[8,64,1024]{2,1,0:T(8,128)(2,1)}), bf16[8,64,1024]{2,1,0:T(8,128)(2,1)S(1)}, u32[]{:S(2)}, u32[]{:S(2)}) async-start(bf16[8,64,1024]{2,1,0:T(8,128)(2,1)} %bitcast.54), calls=%async_computation.6 | async-start | bytes 2097152 | tf_op jit(solution)/shard_map/all_to_all | solution.py:28
  26.8 21.1 %copy-start.12 = (f32[1024]{0:T(1024)S(1)}, f32[1024]{0:T(1024)}, u32[]{:S(2)}) copy-start(f32[1024]{0:T(1024)} %param.8) | copy-start | bytes 12292
  26.8 18.9 %all-to-all-start = ((bf16[8,64,1024]{2,1,0:T(8,128)(2,1)}), bf16[8,64,1024]{2,1,0:T(8,128)(2,1)}, u32[]{:S(2)}, u32[]{:S(2)}) async-start(bf16[8,64,1024]{2,1,0:T(8,128)(2,1)} %bitcast.53), calls=%async_computation | async-start | bytes 2097152 | tf_op jit(solution)/shard_map/all_to_all | solution.py:28
  47.1 0.7 copy-start.4
  49.3 17.2 %all-to-all-start.1 = ((bf16[8,64,1024]{2,1,0:T(8,128)(2,1)}), bf16[8,64,1024]{2,1,0:T(8,128)(2,1)S(1)}, u32[]{:S(2)}, u32[]{:S(2)}) async-start(bf16[8,64,1024]{2,1,0:T(8,128)(2,1)} %broadcast_in_dim.12), calls=%async_computation.1 | async-start | bytes 2097152 | tf_op jit(solution)/shard_map/all_to_all | solution.py:33
  66.5 10.8 %copy-start.1 = (bf16[8,64,1024]{2,1,0:T(8,128)(2,1)}, bf16[8,64,1024]{2,1,0:T(8,128)(2,1)S(1)}, u32[]{:S(2)}) copy-start(bf16[8,64,1024]{2,1,0:T(8,128)(2,1)S(1)} %all-to-all-done.1) | copy-start | bytes 3145732
  67.7 17.0 %all-to-all-start.7 = ((bf16[8,64,1024]{2,1,0:T(8,128)(2,1)}), bf16[8,64,1024]{2,1,0:T(8,128)(2,1)}, u32[]{:S(2)}, u32[]{:S(2)}) async-start(bf16[8,64,1024]{2,1,0:T(8,128)(2,1)} %broadcast_in_dim.15), calls=%async_computation.7 | async-start | bytes 2097152 | tf_op jit(solution)/shard_map/all_to_all | solution.py:33
  75.1 2.3 collective-permute-start
  84.7 23.3 %all-to-all-start.2 = ((bf16[16,16,1024]{2,1,0:T(8,128)(2,1)}), bf16[16,16,1024]{2,1,0:T(8,128)(2,1)S(1)}, u32[]{:S(2)}, u32[]{:S(2)}) async-start(bf16[16,16,1024]{2,1,0:T(8,128)(2,1)} %bitcast.56), calls=%async_computation.2 | async-start | bytes 1048576 | tf_op jit(solution)/shard_map/all_to_all | solution.py:28
  95.5 4.6 %copy-start.5 = (bf16[1024,1024]{1,0:T(8,128)(2,1)S(1)}, bf16[1024,1024]{1,0:T(8,128)(2,1)}, u32[]{:S(2)}) copy-start(bf16[1024,1024]{1,0:T(8,128)(2,1)} %param.7) | copy-start | bytes 6291460
  98.1 2.0 collective-permute-start.5
  102.7 26.7 %copy-start.13 = (f32[1024]{0:T(1024)S(1)}, f32[1024]{0:T(1024)}, u32[]{:S(2)}) copy-start(f32[1024]{0:T(1024)} %param.9) | copy-start | bytes 12292
  108.1 21.2 %all-to-all-start.8 = ((bf16[16,16,1024]{2,1,0:T(8,128)(2,1)}), bf16[16,16,1024]{2,1,0:T(8,128)(2,1)S(1)}, u32[]{:S(2)}, u32[]{:S(2)}) async-start(bf16[16,16,1024]{2,1,0:T(8,128)(2,1)} %bitcast.55), calls=%async_computation.8 | async-start | bytes 1048576 | tf_op jit(solution)/shard_map/all_to_all | solution.py:28
  151.1 20.7 %all-to-all-start.3 = ((bf16[16,16,1024]{2,1,0:T(8,128)(2,1)}), bf16[16,16,1024]{2,1,0:T(8,128)(2,1)}, u32[]{:S(2)}, u32[]{:S(2)}) async-start(bf16[16,16,1024]{2,1,0:T(8,128)(2,1)} %broadcast_in_dim.13), calls=%async_computation.3 | async-start | bytes 1048576 | tf_op jit(solution)/shard_map/all_to_all | solution.py:33
  156.6 15.2 %collective-permute-start.6 = (bf16[256,1024]{1,0:T(8,128)(2,1)S(1)}, bf16[256,1024]{1,0:T(8,128)(2,1)S(1)}, u32[]{:S(2)}, u32[]{:S(2)}) collective-permute-start(bf16[256,1024]{1,0:T(8,128)(2,1)S(1)} %bitcast.49), channel_id=1, source_target_pairs={{0,1},{1,0},{2,3},{3,2},{4,5},{5,4},{6,7},{7,6},{8,9},{9,8},{10,11... | collective-permute-start | bytes 1572872 | tf_op jit(solution)/shard_map/ppermute | solution.py:23
  171.8 2.0 copy-start.6
  171.8 8.7 %collective-permute-start.1 = (bf16[256,1024]{1,0:T(8,128)(2,1)}, bf16[256,1024]{1,0:T(8,128)(2,1)}, u32[]{:S(2)}, u32[]{:S(2)}) collective-permute-start(bf16[256,1024]{1,0:T(8,128)(2,1)} %bitcast.5), channel_id=1, source_target_pairs={{0,1},{1,0},{2,3},{3,2},{4,5},{5,4},{6,7},{7,6},{8,9},{9,8},{10,11... | collective-permute-start | bytes 1572872 | tf_op jit(solution)/shard_map/ppermute | solution.py:23
  171.9 4.1 %copy-start.8 = (bf16[256,1024]{1,0:T(8,128)(2,1)}, bf16[256,1024]{1,0:T(8,128)(2,1)S(1)}, u32[]{:S(2)}) copy-start(bf16[256,1024]{1,0:T(8,128)(2,1)S(1)} %get-tuple-element.12) | copy-start | bytes 1572868
  171.9 4.1 %copy-start.9 = (bf16[256,1024]{1,0:T(8,128)(2,1)}, bf16[256,1024]{1,0:T(8,128)(2,1)S(1)}, u32[]{:S(2)}) copy-start(bf16[256,1024]{1,0:T(8,128)(2,1)S(1)} %get-tuple-element.13) | copy-start | bytes 1572868
  176.0 19.0 %all-to-all-start.10 = ((bf16[8,64,1024]{2,1,0:T(8,128)(2,1)}), bf16[8,64,1024]{2,1,0:T(8,128)(2,1)S(1)}, u32[]{:S(2)}, u32[]{:S(2)}) async-start(bf16[8,64,1024]{2,1,0:T(8,128)(2,1)} %bitcast.52), calls=%async_computation.10 | async-start | bytes 2097152 | tf_op jit(solution)/shard_map/all_to_all | solution.py:28
  180.5 2.4 copy-start.7
  181.9 0.8 copy-start.10
  181.9 1.0 copy-start.11
  195.1 26.2 %all-to-all-start.4 = ((bf16[8,64,1024]{2,1,0:T(8,128)(2,1)}), bf16[8,64,1024]{2,1,0:T(8,128)(2,1)}, u32[]{:S(2)}, u32[]{:S(2)}) async-start(bf16[8,64,1024]{2,1,0:T(8,128)(2,1)} %bitcast.50), calls=%async_computation.4 | async-start | bytes 2097152 | tf_op jit(solution)/shard_map/all_to_all | solution.py:28
  199.5 13.1 %copy-start.2 = (bf16[8,64,1024]{2,1,0:T(8,128)(2,1)S(1)}, bf16[8,64,1024]{2,1,0:T(8,128)(2,1)}, u32[]{:S(2)}) copy-start(bf16[8,64,1024]{2,1,0:T(8,128)(2,1)} %copy-done.1) | copy-start | bytes 3145732
  201.7 9.9 %collective-permute-start.2 = (f32[1024]{0:T(1024)S(1)}, f32[1024]{0:T(1024)S(1)}, u32[]{:S(2)}, u32[]{:S(2)}) collective-permute-start(f32[1024]{0:T(1024)S(1)} %fusion), channel_id=1, source_target_pairs={{0,32},{32,0},{1,33},{33,1},{2,34},{34,2},{3,35},{35,3},{4,36},{36... | collective-permute-start | bytes 12296 | tf_op jit(solution)/shard_map/ppermute | solution.py:23
  211.6 3.6 %collective-permute-start.3 = (f32[1024]{0:T(1024)S(1)}, f32[1024]{0:T(1024)S(1)}, u32[]{:S(2)}, u32[]{:S(2)}) collective-permute-start(f32[1024]{0:T(1024)S(1)} %add.153), channel_id=1, source_target_pairs={{0,64},{64,0},{128,192},{192,128},{1,65},{65,1},{129,193},{193,129... | collective-permute-start | bytes 12296 | tf_op jit(solution)/shard_map/ppermute | solution.py:23
  215.2 5.2 %collective-permute-start.4 = (f32[1024]{0:T(1024)S(1)}, f32[1024]{0:T(1024)S(1)}, u32[]{:S(2)}, u32[]{:S(2)}) collective-permute-start(f32[1024]{0:T(1024)S(1)} %get-tuple-element.7), channel_id=1, source_target_pairs={{0,128},{64,192},{128,0},{192,64},{1,129},{65,193},{129,1},{193,65... | collective-permute-start | bytes 12296 | tf_op jit(solution)/shard_map/ppermute | solution.py:23
  239.7 5.3 %copy-start.3 = (bf16[8,64,1024]{2,1,0:T(8,128)(2,1)S(1)}, bf16[8,64,1024]{2,1,0:T(8,128)(2,1)}, u32[]{:S(2)}) copy-start(bf16[8,64,1024]{2,1,0:T(8,128)(2,1)} %copy-done.1) | copy-start | bytes 3145732
  240.8 15.8 %all-to-all-start.11 = ((bf16[8,64,1024]{2,1,0:T(8,128)(2,1)}), bf16[8,64,1024]{2,1,0:T(8,128)(2,1)}, u32[]{:S(2)}, u32[]{:S(2)}) async-start(bf16[8,64,1024]{2,1,0:T(8,128)(2,1)} %broadcast_in_dim.17), calls=%async_computation.11 | async-start | bytes 2097152 | tf_op jit(solution)/shard_map/all_to_all | solution.py:33
